TPU v7x, 256 devices: a whole 4x4x8 slice. The times are simulated.
256 devices in a mesh: gene: 4 (over z_hi), cell: 64 (over x, y, z_lo, core).
Axes of the slice: x: 4, y: 4, z: 8 (z_hi: 4, z_lo: 2; z = z_hi * 2 + z_lo), core: 2. Of those that a mesh axis runs over, the one named last changes fastest.
Arguments:
- counts: int32 [16384, 32768], P('gene', 'cell'), may hold values from 0 to 2047, as said below
- w1: bfloat16 [16384, 512], P(('gene', 'cell')), may hold values from 0.099609375 to 2
- h1: float32 [512, 32768], P(None, 'cell'), may hold values from 0.1 to 2
- w2: float32 [512, 64], replicated, may hold values from 0.1 to 2
- h2: float32 [64, 32768], P(None, 'cell'), may hold values from 0.005 to 0.1
Outputs:
- w1_new: bfloat16 [16384, 512], P(('gene', 'cell'))
- h1_new: float32 [512, 32768], P(None, 'cell')
- w2_new: float32 [512, 64], replicated
- h2_new: float32 [64, 32768], P(None, 'cell')
Inputs may be any that keep to these rules, and one draw needn't show every extreme that they name: `counts`: counts are whole numbers; a gene's and a cell's typical depth vary, and cells later in the order run deeper.
All inputs are finite; a program needn't handle non-finite values.
Results may differ from a plain program's by a relative error of at most 0.0013.
The roundings to bfloat16 on the way count: a program that leaves them out, or rounds other values in their place, can miss the bound.
Values may be sent and summed in bfloat16 or wider, within the bound.
A program may use at most 64 MiB of HBM per device.

v0:
```python
import jax
import jax.numpy as jnp
from jax import lax
from jax.sharding import PartitionSpec as P


def layer_two(h1_new, w2, h2):
    hi = lax.Precision.HIGHEST
    ratio3 = h1_new / jnp.dot(w2, h2, precision=hi)
    h2_new = h2 * jnp.dot(w2.T, ratio3, precision=hi) / jnp.sum(w2, axis=0)[:, None]
    ratio4 = h1_new / jnp.dot(w2, h2_new, precision=hi)
    w2_part = jnp.dot(ratio4, h2_new.T, precision=hi)
    h2_part = jnp.sum(h2_new, axis=1)
    return (h2_new, w2_part, h2_part)


def on_device(counts, w1, h1, w2, h2):
    w1_block = lax.all_gather(w1, "cell", axis=0, tiled=True)
    values = counts.astype(jnp.float32)
    h1_low = h1.astype(jnp.bfloat16)
    approx = jnp.dot(w1_block, h1_low, preferred_element_type=jnp.float32)
    ratio = (values / approx).astype(jnp.bfloat16)
    partial_num = lax.dot_general(
        w1_block, ratio, (((0,), (0,)), ((), ())), preferred_element_type=jnp.float32
    )
    partial_col = jnp.sum(w1_block.astype(jnp.float32), axis=0)
    h1_num, colsum = lax.psum((partial_num, partial_col), "gene")
    h1_new = h1 * h1_num / colsum[:, None]
    h1_low2 = h1_new.astype(jnp.bfloat16)
    approx2 = jnp.dot(w1_block, h1_low2, preferred_element_type=jnp.float32)
    ratio2 = (values / approx2).astype(jnp.bfloat16)
    local_rows = jnp.sum(h1_new, axis=1)
    rowsum = lax.psum(local_rows, "cell")
    w1_num = lax.psum_scatter(
        lax.dot_general(
            ratio2, h1_low2, (((1,), (1,)), ((), ())), preferred_element_type=jnp.float32
        ),
        "cell",
        scatter_dimension=0,
        tiled=True,
    )
    w1_new = (w1.astype(jnp.float32) * w1_num / rowsum[None, :]).astype(jnp.bfloat16)
    h2_new, w2_part, h2_part = layer_two(h1_new, w2, h2)
    w2_num, h2_rows = lax.psum((w2_part, h2_part), "cell")
    w2_new = w2 * w2_num / h2_rows[None, :]
    return (w1_new, h1_new, w2_new, h2_new)


def solution(mesh):
    placed = (P("gene", "cell"), P(("gene", "cell"), None), P(None, "cell"), P(), P(None, "cell"))
    return jax.shard_map(
        on_device,
        mesh=mesh,
        in_specs=placed,
        out_specs=(P(("gene", "cell"), None), P(None, "cell"), P(), P(None, "cell")),
        check_vma=False,
    )
```

profile of v0, /device:TPU:64, one launch (start us, length us, event | category | flops | bytes accessed | tf_op | source)
XLA Modules:
  0.0 999.0 jit_solution(18031313151263550134)
XLA Ops:
  7.2 0.0 all-gather.2.cloned.1.call-start
  7.2 0.7 all-gather.2.cloned.1.call-update
  7.9 0.0 all-reduce.4.cloned.1.call-start
  8.0 112.6 %all-gather.2.cloned.1.call-done = bf16[4096,512]{1,0:T(8,128)(2,1)} async-done(((bf16[64,512]{1,0:T(8,128)(2,1)}), bf16[4096,512]{1,0:T(8,128)(2,1)}) %all-gather.2.cloned.1.call-update) | async-done | bytes 4194320 | tf_op jit(solution)/shard_map/all_gather | solution.py:18
  120.6 11.9 %fusion.8 = f32[512,512]{0,1:T(8,128)} fusion(bf16[4096,512]{1,0:T(8,128)(2,1)} %all-gather.2.cloned.1.call-done, s32[4096,512]{1,0:T(8,128)} %param.5, f32[512,512]{1,0:T(8,128)} %param.7), kind=kOutput, calls=%fused_computation.12 | convolution fusion | flops 4301520896 | bytes 14680064 | tf_op jit(solution)/shard_map/dot_general | solution.py:23
  132.6 0.0 all-reduce.6.cloned.1.call-start
  132.6 0.3 copy.9
  133.0 0.1 reduce_sum.38
  133.1 2.8 convert_reduce_fusion
  135.9 11.2 %psum.36 = f32[512]{0:T(512)S(1)} all-reduce(f32[512]{0:T(512)S(1)} %convert_reduce_fusion), channel_id=1, replica_groups=mesh['gene'=4,'cell'=64] {'gene'}, use_global_device_ids=true, to_apply=%region_2.0 | all-reduce | flops 512 | bytes 4096 | tf_op jit(solution)/shard_map/psum | solution.py:27
  147.1 50.6 %all-reduce.4.cloned.1.call-done = f32[512,512]{0,1:T(8,128)} async-done(((f32[512,512]{0,1:T(8,128)}), f32[512,512]{0,1:T(8,128)}) %all-reduce.4.cloned.1.call-update) | async-done | bytes 1048592 | tf_op jit(solution)/shard_map/psum | solution.py:27
  197.7 2.5 fusion.6
  200.2 1.2 fusion.16
  201.4 1.2 fusion.7
  202.6 1.5 fusion.17
  204.1 0.2 reduce-scatter.2.cloned.1.call-start
  204.3 0.3 fusion.15
  204.6 12.5 %fusion.4 = f32[4096,512]{1,0:T(8,128)} fusion(s32[4096,512]{1,0:T(8,128)} %param.5, bf16[4096,512]{1,0:T(8,128)(2,1)} %all-gather.2.cloned.1.call-done, f32[512,512]{0,1:T(8,128)S(1)} %get-tuple-element.11), kind=kOutput, calls=%fused_computation.6 | convolution fusion | flops 4301783040 | bytes 22020096 | tf_op jit(solution)/shard_map/dot_general | solution.py:35
  217.1 1.3 copy.10
  218.4 142.9 %all-reduce = (f32[512]{0:T(512)S(1)}, f32[64]{0:T(128)S(1)}) all-reduce(f32[512]{0:T(512)S(1)} %get-tuple-element.10, f32[64]{0:T(128)S(1)} %get-tuple-element.12), channel_id=1, replica_groups=mesh['gene'=4,'cell'=64] {'cell'}, use_global_device_ids=true, to_apply=%region_5.0 | all-reduce | flops 576 | bytes 4608 | tf_op jit(solution)/shard_map/psum | solution.py:33
  361.3 328.9 %all-reduce.6.cloned.1.call-done = f32[512,64]{0,1:T(8,128)} async-done(((f32[512,64]{0,1:T(8,128)}), f32[512,64]{0,1:T(8,128)}) %all-reduce.6.cloned.1.call-update) | async-done | bytes 131088 | tf_op jit(solution)/shard_map/psum | solution.py:44
  690.2 1.6 multiply_divide_fusion
  691.9 299.1 %reduce-scatter.2.cloned.1.call-done = f32[64,512]{1,0:T(8,128)} async-done(((f32[4096,512]{1,0:T(8,128)}), f32[64,512]{1,0:T(8,128)}) %reduce-scatter.2.cloned.1.call-update) | async-done | bytes 131088 | tf_op jit(solution)/shard_map/reduce_scatter | solution.py:34
  990.9 1.6 divide_convert_fusion.4
  (15 shorter events, 0.1 us)
Async XLA Ops:
  7.2 113.4 %all-gather.2.cloned.1.call-start = ((), (), s32[]{:S(2)}) async-start(), calls=%async_computation.1 | async-start | bytes 4259840 | tf_op jit(solution)/shard_map/all_gather | solution.py:18
  7.9 124.7 %copy-start.1 = (f32[512,512]{1,0:T(8,128)S(1)}, f32[512,512]{1,0:T(8,128)}, u32[]{:S(2)}) copy-start(f32[512,512]{1,0:T(8,128)} %param.7) | copy-start | bytes 3145732
  7.9 125.1 %copy-start = (f32[512,64]{0,1:T(8,128)S(1)}, f32[512,64]{0,1:T(8,128)}, u32[]{:S(2)}) copy-start(f32[512,64]{0,1:T(8,128)} %param.8) | copy-start | bytes 393220
  7.9 189.8 %all-reduce.4.cloned.1.call-start = ((), (), s32[]{:S(2)}) async-start(), calls=%async_computation.2 | async-start | bytes 2097152 | tf_op jit(solution)/shard_map/psum | solution.py:27
  132.5 65.2 %copy-start.5 = (f32[64,512]{1,0:T(8,128)S(1)}, f32[64,512]{1,0:T(8,128)}, u32[]{:S(2)}) copy-start(f32[64,512]{1,0:T(8,128)} %param.9) | copy-start | bytes 393220
  132.6 557.7 %all-reduce.6.cloned.1.call-start = ((), (), s32[]{:S(2)}) async-start(), calls=%async_computation.4 | async-start | bytes 262144 | tf_op jit(solution)/shard_map/psum | solution.py:44
  197.7 3.7 copy-start.2
  201.4 3.2 copy-start.3
  204.1 786.8 %reduce-scatter.2.cloned.1.call-start = ((), (), s32[]{:S(2)}) async-start(), calls=%async_computation.3 | async-start | bytes 8519680 | tf_op jit(solution)/shard_map/reduce_scatter | solution.py:34
  217.1 773.8 %copy-start.4 = (bf16[64,512]{1,0:T(8,128)(2,1)S(1)}, bf16[64,512]{1,0:T(8,128)(2,1)}, u32[]{:S(2)}) copy-start(bf16[64,512]{1,0:T(8,128)(2,1)} %param.6) | copy-start | bytes 196612
Sparse Core Ops, SparseCore 0:
  9.9 110.7 all-gather.1
  132.7 64.9 all-reduce.3
  204.2 485.9 all-reduce.5
  692.6 298.2 reduce-scatter.1
where the time goes:
time: 999 us
  waiting for transfers between devices  792 us (79%)
  blocking collectives  154 us (15%)
  matrix products  30.7 us (3%)
  between operations  13.8 us (1%)
    psum x1, waiting for transfers between devices, on_device(): w2_num, h2_rows = lax.psum((w2_part, h2_part), 'cell')  329 us
    reduce_scatter x1, waiting for transfers between devices, on_device(): lax.psum_scatter(lax.dot_general(ratio2, h1_low2, (((1,), (1,)), ((), ())...  299 us
    psum x1, blocking collectives, on_device(): rowsum = lax.psum(local_rows, 'cell')  143 us
    all_gather x1, waiting for transfers between devices, on_device(): w1_block = lax.all_gather(w1, 'cell', axis=0, tiled=True)  113 us
    psum x1, waiting for transfers between devices, on_device(): h1_num, colsum = lax.psum((partial_num, partial_col), 'gene')  50.6 us
  transfers between devices with their start and end apart: 4, of which 4 were waited for; matrix products, arithmetic and copies ran while one was open for 2% of the time, Pallas kernels for 0%

commit v1 on v0

--- a/solution.py
+++ b/solution.py
@@ -15,7 +15,9 @@
 
 
 def on_device(counts, w1, h1, w2, h2):
-    w1_block = lax.all_gather(w1, "cell", axis=0, tiled=True)
+    w1_block = jnp.concatenate(
+        lax.all_to_all(jnp.stack([w1] * lax.axis_size("cell")), "cell", 0, 0), axis=0
+    )
     values = counts.astype(jnp.float32)
     h1_low = h1.astype(jnp.bfloat16)
     approx = jnp.dot(w1_block, h1_low, preferred_element_type=jnp.float32)

time: 999 us -> 949 us (0.950)
  waiting for transfers between devices: 792 us -> 679 us
  blocking collectives: 154 us -> 215 us
    all_gather x1 -> x0, waiting for transfers between devices: 113 us -> none  [on_device(): w1_block = lax.all_gather(w1, 'cell', axis=0, tiled=True)]
    all_to_all x0 -> x1, blocking collectives: none -> 61.2 us  [on_device(): lax.all_to_all(jnp.stack([w1] * lax.axis_size('cell')), 'cell', 0, 0)]
  transfers between devices with their start and end apart: 4 -> 3, of which waited for: 4 -> 3; matrix products, arithmetic and copies ran while one was open for 2% -> 2% of each run, Pallas kernels for 0% -> 0%
where the time goes in v1:
time: 949 us; the launch traced here: 948 us
  waiting for transfers between devices  679 us (72%)
  blocking collectives  215 us (23%)
  matrix products  30.4 us (3%)
  between operations  13.8 us (1%)
    psum x1, waiting for transfers between devices, on_device(): w2_num, h2_rows = lax.psum((w2_part, h2_part), 'cell')  329 us
    reduce_scatter x1, waiting for transfers between devices, on_device(): lax.psum_scatter(lax.dot_general(ratio2, h1_low2, (((1,), (1,)), ((), ())...  299 us
    psum x1, blocking collectives, on_device(): rowsum = lax.psum(local_rows, 'cell')  143 us
    all_to_all x1, blocking collectives, on_device(): lax.all_to_all(jnp.stack([w1] * lax.axis_size('cell')), 'cell', 0, 0)  61.2 us
    psum x1, waiting for transfers between devices, on_device(): h1_num, colsum = lax.psum((partial_num, partial_col), 'gene')  50.7 us
  transfers between devices with their start and end apart: 3, of which 3 were waited for; matrix products, arithmetic and copies ran while one was open for 2% of the time, Pallas kernels for 0%

profile of v1, /device:TPU:64, one launch (start us, length us, event | category | flops | bytes accessed | tf_op | source)
XLA Modules:
  0.0 948.2 jit_solution(10383549977356017198)
XLA Ops:
  7.2 0.0 all-reduce.4.cloned.1.call-start
  7.2 1.3 stack.2
  8.6 61.2 %all_to_all.5 = bf16[64,64,512]{2,1,0:T(8,128)(2,1)} all-to-all(bf16[64,64,512]{2,1,0:T(8,128)(2,1)S(1)} %stack.2), channel_id=1, replica_groups=mesh['gene'=4,'cell'=64] {'cell'}, dimensions={0} | all-to-all | bytes 8388608 | tf_op jit(solution)/shard_map/all_to_all | solution.py:19
  69.8 11.6 %fusion.8 = f32[512,512]{0,1:T(8,128)} fusion(bf16[4096,512]{1,0:T(8,128)(2,1)} %bitcast.30, s32[4096,512]{1,0:T(8,128)} %param.5, f32[512,512]{1,0:T(8,128)S(1)} %copy-done.1), kind=kOutput, calls=%fused_computation.12 | convolution fusion | flops 4301520896 | bytes 14680064 | tf_op jit(solution)/shard_map/dot_general | solution.py:25
  81.3 0.0 all-reduce.4.cloned.1.call-update
  81.4 0.0 all-reduce.6.cloned.1.call-start
  81.4 0.3 copy.11
  81.8 0.1 reduce_sum.38
  81.9 2.8 convert_reduce_fusion
  84.7 11.4 %psum.36 = f32[512]{0:T(512)S(1)} all-reduce(f32[512]{0:T(512)S(1)} %convert_reduce_fusion), channel_id=1, replica_groups=mesh['gene'=4,'cell'=64] {'gene'}, use_global_device_ids=true, to_apply=%region_2.0 | all-reduce | flops 512 | bytes 4096 | tf_op jit(solution)/shard_map/psum | solution.py:29
  96.1 50.7 %all-reduce.4.cloned.1.call-done = f32[512,512]{0,1:T(8,128)} async-done(((f32[512,512]{0,1:T(8,128)}), f32[512,512]{0,1:T(8,128)}) %all-reduce.4.cloned.1.call-update) | async-done | bytes 1048592 | tf_op jit(solution)/shard_map/psum | solution.py:29
  146.8 2.5 fusion.6
  149.3 1.2 fusion.16
  150.5 1.2 fusion.7
  151.7 1.5 fusion.17
  153.2 0.2 reduce-scatter.2.cloned.1.call-start
  153.4 0.3 fusion.15
  153.7 12.5 %fusion.4 = f32[4096,512]{1,0:T(8,128)} fusion(s32[4096,512]{1,0:T(8,128)} %param.5, bf16[4096,512]{1,0:T(8,128)(2,1)} %bitcast.31, f32[512,512]{0,1:T(8,128)S(1)} %get-tuple-element.15), kind=kOutput, calls=%fused_computation.6 | convolution fusion | flops 4301783040 | bytes 22020096 | tf_op jit(solution)/shard_map/dot_general | solution.py:37
  166.2 1.3 copy.12
  167.5 142.9 %all-reduce = (f32[512]{0:T(512)S(1)}, f32[64]{0:T(128)S(1)}) all-reduce(f32[512]{0:T(512)S(1)} %get-tuple-element.14, f32[64]{0:T(128)S(1)} %get-tuple-element.16), channel_id=1, replica_groups=mesh['gene'=4,'cell'=64] {'cell'}, use_global_device_ids=true, to_apply=%region_5.0 | all-reduce | flops 576 | bytes 4608 | tf_op jit(solution)/shard_map/psum | solution.py:35
  310.4 328.9 %all-reduce.6.cloned.1.call-done = f32[512,64]{0,1:T(8,128)} async-done(((f32[512,64]{0,1:T(8,128)}), f32[512,64]{0,1:T(8,128)}) %all-reduce.6.cloned.1.call-update) | async-done | bytes 131088 | tf_op jit(solution)/shard_map/psum | solution.py:46
  639.3 1.6 multiply_divide_fusion
  640.9 299.2 %reduce-scatter.2.cloned.1.call-done = f32[64,512]{1,0:T(8,128)} async-done(((f32[4096,512]{1,0:T(8,128)}), f32[64,512]{1,0:T(8,128)}) %reduce-scatter.2.cloned.1.call-update) | async-done | bytes 131088 | tf_op jit(solution)/shard_map/reduce_scatter | solution.py:36
  940.1 1.6 divide_convert_fusion.4
  (14 shorter events, 0.1 us)
Async XLA Ops:
  7.2 139.6 %all-reduce.4.cloned.1.call-start = ((), (), s32[]{:S(2)}) async-start(), calls=%async_computation.2 | async-start | bytes 2097152 | tf_op jit(solution)/shard_map/psum | solution.py:29
  8.6 61.2 %copy-start.1 = (f32[512,512]{1,0:T(8,128)S(1)}, f32[512,512]{1,0:T(8,128)}, u32[]{:S(2)}) copy-start(f32[512,512]{1,0:T(8,128)} %param.7) | copy-start | bytes 3145732
  69.8 12.0 %copy-start = (f32[512,64]{0,1:T(8,128)S(1)}, f32[512,64]{0,1:T(8,128)}, u32[]{:S(2)}) copy-start(f32[512,64]{0,1:T(8,128)} %param.8) | copy-start | bytes 393220
  81.3 65.4 %copy-start.5 = (f32[64,512]{1,0:T(8,128)S(1)}, f32[64,512]{1,0:T(8,128)}, u32[]{:S(2)}) copy-start(f32[64,512]{1,0:T(8,128)} %param.9) | copy-start | bytes 393220
  81.4 557.9 %all-reduce.6.cloned.1.call-start = ((), (), s32[]{:S(2)}) async-start(), calls=%async_computation.4 | async-start | bytes 262144 | tf_op jit(solution)/shard_map/psum | solution.py:46
  146.8 3.7 copy-start.2
  150.5 3.2 copy-start.3
  153.2 786.9 %reduce-scatter.2.cloned.1.call-start = ((), (), s32[]{:S(2)}) async-start(), calls=%async_computation.3 | async-start | bytes 8519680 | tf_op jit(solution)/shard_map/reduce_scatter | solution.py:36
  166.2 774.0 %copy-start.4 = (bf16[64,512]{1,0:T(8,128)(2,1)S(1)}, bf16[64,512]{1,0:T(8,128)(2,1)}, u32[]{:S(2)}) copy-start(bf16[64,512]{1,0:T(8,128)(2,1)} %param.6) | copy-start | bytes 196612
Sparse Core Ops, SparseCore 0:
  81.5 65.2 all-reduce.3
  153.3 485.9 all-reduce.5
  641.8 298.2 reduce-scatter.1
